TPU v7x, 256 devices: a whole 4x4x8 slice. The times are simulated.
256 devices in a mesh: rows: 64 (over z, y, core), feat: 4 (over x).
Axes of the slice: x: 4, y: 4, z: 8, core: 2. Of those that a mesh axis runs over, the one named last changes fastest.
Arguments:
- bin_codes: int32 [16, 983040], P(None, 'rows'), may hold values from 0 to 255
- node_ids: int32 [983040], P('rows'), may hold values from 0 to 7, as said below
- labels: float32 [983040], P('rows'), may hold values from -1 to 1, as said below
- weights: float32 [983040], P('rows'), as said below
- predictions: float32 [983040], P('rows'), may hold values from -6 to 6
- level3_feature: int32 [8], replicated, may hold values from 0 to 15
- level3_bin: int32 [8], replicated, may hold values from 64 to 191
- level4_feature: int32 [16], replicated, may hold values from 0 to 15
- level4_bin: int32 [16], replicated, may hold values from 64 to 191
Outputs:
- level3_hist: float32 [16, 16, 256], P('feat')
- level4_hist: float32 [16, 32, 256], P('feat')
- leaf_values: float32 [32], replicated
- new_predictions: float32 [983040], P('rows')
- new_weights: float32 [983040], P('rows')
Inputs may be any that keep to these rules, and one draw needn't show every extreme that they name: `node_ids`: node ids of level 3. `labels`: every label is -1 or 1. `weights`: every weight is positive.
All inputs are finite; a program needn't handle non-finite values.
Results may differ from a plain program's by a relative error of at most 0.0003.
Values sent between devices are 32-bit elements; how exact they have to be, the bound alone decides.
A program may use at most 64 MiB of HBM per device.

v0:
```python
import math

import jax
import jax.numpy as jnp
from jax import lax
from jax.sharding import PartitionSpec as P

FEATURES = 16
BINS = 256


def in_blocks(shard, dim, length):
    shape = shard.shape
    blocks = shard.reshape(*shape[:dim], length, shape[dim] // length, *shape[dim + 1 :])
    return jnp.moveaxis(blocks, dim, 0)


def summed_on_arrival(shard, axis, dim):
    length = lax.axis_size(axis)
    blocks = lax.all_to_all(in_blocks(shard, dim, length), axis, 0, 0, tiled=True)
    return jnp.sum(blocks, axis=0)


def in_order(blocks, dim):
    blocks = jnp.moveaxis(blocks, 0, dim)
    shape = blocks.shape
    return blocks.reshape(*shape[:dim], shape[dim] * shape[dim + 1], *shape[dim + 2 :])


def copy_for_each(shard, axis):
    length = lax.axis_size(axis)
    return lax.all_to_all(
        jnp.broadcast_to(shard[None], (length, *shard.shape)), axis, 0, 0, tiled=True
    )


def collect(shard, axis, dim):
    return in_order(copy_for_each(shard, axis), dim)


def over_copies(shard, axis):
    return copy_for_each(shard, axis).sum(axis=0)


def in_one(arrays, axis):
    flat, at, outs = (jnp.concatenate([a.reshape(-1) for a in arrays]), 0, [])
    so_far = over_copies(flat, axis)
    for a in arrays:
        outs.append(so_far[at : at + a.size].reshape(a.shape))
        at += a.size
    return tuple(outs)


def routing(bin_codes, node_of, features, thresholds):
    node_count = features.shape[0]
    member = node_of[:, None] == jnp.arange(node_count, dtype=jnp.int32)[None, :]
    chosen = jnp.sum(jnp.where(member, features[None, :], 0), axis=1)
    cutoff = jnp.sum(jnp.where(member, thresholds[None, :], 0), axis=1)
    all_ids = jnp.arange(bin_codes.shape[0], dtype=jnp.int32)
    owner_mask = chosen[None, :] == all_ids[:, None]
    picked = jnp.sum(jnp.where(owner_mask, bin_codes, 0), axis=0)
    return (picked > cutoff).astype(jnp.int32)


def partial_histogram(bin_codes, node_of, node_count, weight_bf, signed_bf):
    feature_local = bin_codes.shape[0]
    row_count = node_of.shape[0]
    block_rows = math.gcd(row_count, 1024)
    turns = row_count // block_rows
    code_blocks = bin_codes.reshape(feature_local, turns, block_rows).transpose(1, 0, 2)
    node_blocks = node_of.reshape(turns, block_rows)
    weight_blocks = weight_bf.reshape(turns, block_rows)
    signed_blocks = signed_bf.reshape(turns, block_rows)
    bin_range = jnp.arange(BINS, dtype=jnp.int32)
    node_range = jnp.arange(node_count, dtype=jnp.int32)

    def accumulate(running, pieces):
        code_piece, node_piece, weight_piece, signed_piece = pieces
        member = node_piece[:, None] == node_range[None, :]
        nothing = jnp.zeros((), jnp.bfloat16)
        row_matrix = jnp.concatenate(
            [
                jnp.where(member, weight_piece[:, None], nothing),
                jnp.where(member, signed_piece[:, None], nothing),
            ],
            axis=1,
        )
        onehot_bins = (code_piece[:, :, None] == bin_range[None, None, :]).astype(jnp.bfloat16)
        return (
            running
            + jnp.einsum(
                "rn,frb->fnb", row_matrix, onehot_bins, preferred_element_type=jnp.float32
            ),
            None,
        )

    initial = jnp.zeros((feature_local, 2 * node_count, BINS), jnp.float32)
    running, _ = lax.scan(
        accumulate, initial, (code_blocks, node_blocks, weight_blocks, signed_blocks)
    )
    return running


def combine_rows(partial_value):
    shares = summed_on_arrival(partial_value, "rows", 2)
    return collect(shares, "rows", 2)


def on_device(
    bin_codes,
    node_ids,
    labels,
    weights,
    predictions,
    level3_feature,
    level3_bin,
    level4_feature,
    level4_bin,
):
    feature_local = FEATURES // lax.axis_size("feat")
    feat_position = lax.axis_index("feat")
    feature_base = feat_position * feature_local
    own_codes = lax.dynamic_slice_in_dim(bin_codes, feature_base, feature_local, 0)
    weight_bf = weights.astype(jnp.bfloat16)
    signed_bf = (weights * labels).astype(jnp.bfloat16)
    parents = level3_feature.shape[0]
    parent_partial = partial_histogram(own_codes, node_ids, parents, weight_bf, signed_bf)
    go_three = routing(bin_codes, node_ids, level3_feature, level3_bin)
    node_four = 2 * node_ids + go_three
    second_count = 2 * parents
    child_partial = partial_histogram(own_codes, node_four, second_count, weight_bf, signed_bf)
    level3_hist = combine_rows(parent_partial)
    child_hist = combine_rows(child_partial)
    go_four = routing(bin_codes, node_four, level4_feature, level4_bin)
    leaf_of = 2 * node_four + go_four
    nodes_four = level4_feature.shape[0]
    leaf_count = 2 * nodes_four
    local_slot = level4_feature % feature_local
    owner_flag = jnp.repeat(level4_feature // feature_local == feat_position, 2)
    picked = child_hist[local_slot]
    positions = jnp.arange(nodes_four, dtype=jnp.int32)
    weight_rows = picked[positions, positions]
    signed_rows = picked[positions, nodes_four + positions]
    below = jnp.arange(BINS, dtype=jnp.int32)[None, :] <= level4_bin[:, None]

    def split_sums(hist_rows):
        left_sum = jnp.sum(jnp.where(below, hist_rows, 0.0), axis=1)
        whole_sum = jnp.sum(hist_rows, axis=1)
        paired = jnp.stack([left_sum, whole_sum - left_sum], axis=1).reshape(-1)
        return jnp.where(owner_flag, paired, 0.0)

    leaf_weight, leaf_signed = in_one((split_sums(weight_rows), split_sums(signed_rows)), "feat")
    leaf_values = leaf_signed / (leaf_weight + 1.0)
    leaf_match = leaf_of[:, None] == jnp.arange(leaf_count, dtype=jnp.int32)[None, :]
    stepped = jnp.sum(jnp.where(leaf_match, leaf_values[None, :], 0.0), axis=1)
    new_predictions = predictions + stepped
    raw_weights = weights * jnp.exp(-labels * stepped)
    grand_sum = over_copies(jnp.sum(raw_weights), "rows")
    new_weights = raw_weights * (raw_weights.shape[0] * lax.axis_size("rows") / grand_sum)
    return (level3_hist, child_hist, leaf_values, new_predictions, new_weights)


def solution(mesh):
    placed = (P(None, "rows"), P("rows"), P("rows"), P("rows"), P("rows"), P(), P(), P(), P())
    return jax.shard_map(
        on_device,
        mesh=mesh,
        in_specs=placed,
        out_specs=(P("feat", None, None), P("feat", None, None), P(), P("rows"), P("rows")),
        check_vma=False,
    )
```

profile of v0, /device:TPU:1, one launch (start us, length us, event | category | flops | bytes accessed | tf_op | source)
XLA Modules:
  0.0 150.6 jit_solution(1695818442910251859)
XLA Ops:
  0.6 0.9 multiply_convert_fusion
  1.7 0.8 reshape.131
  2.5 1.1 constant_dynamic-slice_fusion.2
  3.6 22.7 %while.22 = (s32[]{:T(128)}, f32[4,16,256]{2,1,0:T(8,128)S(1)}, s32[15,4,1024]{2,1,0:T(4,128)S(1)}, s32[15,1024]{1,0:T(8,128)S(1)}, bf16[15,1024]{1,0:T(8,128)(2...) while((s32[]{:T(128)}, f32[4,16,256]{2,1,0:T(8,128)S(1)}, ...), condition=%wide.region_1.2_spmd.clone, body=%wide.region_0.1_spmd.clone.sunk | while | flops 34725888 | bytes 270451 | solution.py:98
  3.7 1.4 fusion.41
  5.3 1.4 fusion.41
  6.8 1.4 fusion.41
  8.3 1.4 fusion.41
  9.8 1.4 fusion.41
  11.3 1.4 fusion.41
  12.8 1.4 fusion.41
  14.4 1.4 fusion.41
  15.9 1.4 fusion.41
  17.4 1.4 fusion.41
  18.9 1.4 fusion.41
  20.4 1.4 fusion.41
  21.9 1.4 fusion.41
  23.4 1.4 fusion.41
  25.0 1.4 fusion.41
  26.7 1.1 reshape.166
  27.8 13.3 %all-to-all-start = ((f32[64,1,256]{2,1,0:T(1,128)}), f32[64,1,256]{2,1,0:T(1,128)S(1)}, u32[]{:S(2)}, u32[]{:S(2)}) async-start(f32[64,1,256]{2,1,0:T(1,128)} %reshape.166), calls=%async_computation | async-start | bytes 131072 | tf_op jit(solution)/shard_map/all_to_all | solution.py:20
  42.6 24.1 %while.23 = (s32[]{:T(128)}, f32[4,32,256]{2,1,0:T(8,128)S(1)}, s32[15,4,1024]{2,1,0:T(4,128)S(1)}, s32[15,1024]{1,0:T(8,128)S(1)}, bf16[15,1024]{1,0:T(8,128)(2...) while((s32[]{:T(128)}, f32[4,32,256]{2,1,0:T(8,128)S(1)}, ...), condition=%wide.region_7.8_spmd.clone, body=%wide.region_6.7_spmd.clone.sunk | while | flops 68403200 | bytes 467059 | solution.py:98
  42.7 1.5 fusion.43
  44.3 1.5 fusion.43
  45.9 1.5 fusion.43
  47.6 1.5 fusion.43
  49.2 1.5 fusion.43
  50.8 1.5 fusion.43
  52.4 1.5 fusion.43
  54.0 1.5 fusion.43
  55.6 1.5 fusion.43
  57.2 1.5 fusion.43
  58.8 1.5 fusion.43
  60.4 1.5 fusion.43
  62.0 1.5 fusion.43
  63.6 1.5 fusion.43
  65.2 1.5 fusion.43
  67.0 1.0 reshape.170
  68.0 10.3 %all-to-all-start.2 = ((f32[64,1,512]{2,1,0:T(1,128)}), f32[64,1,512]{2,1,0:T(1,128)S(1)}, u32[]{:S(2)}, u32[]{:S(2)}) async-start(f32[64,1,512]{2,1,0:T(1,128)} %reshape.170), calls=%async_computation.2 | async-start | bytes 262144 | tf_op jit(solution)/shard_map/all_to_all | solution.py:20
  78.4 0.5 broadcast.144
  78.9 0.8 reduce.10
  80.1 9.4 %all-to-all-done.2 = f32[64,1,512]{2,1,0:T(1,128)S(1)} async-done(((f32[64,1,512]{2,1,0:T(1,128)}), f32[64,1,512]{2,1,0:T(1,128)S(1)}, u32[]{:S(2)}, u32[]{:S(2)}) %all-to-all-start.2) | async-done | bytes 131104 | tf_op jit(solution)/shard_map/all_to_all | solution.py:20
  89.4 1.0 reduce.12
  90.9 1.0 reshape.172
  91.9 4.4 %all-to-all-start.3 = ((f32[64,1,512]{2,1,0:T(1,128)}), f32[64,1,512]{2,1,0:T(1,128)S(1)}, u32[]{:S(2)}, u32[]{:S(2)}) async-start(f32[64,1,512]{2,1,0:T(1,128)} %reshape.172), calls=%async_computation.3 | async-start | bytes 262144 | tf_op jit(solution)/shard_map/all_to_all | solution.py:32
  96.5 1.1 reshape.168
  97.6 10.1 %all-to-all-done.3 = f32[64,1,512]{2,1,0:T(1,128)S(1)} async-done(((f32[64,1,512]{2,1,0:T(1,128)}), f32[64,1,512]{2,1,0:T(1,128)S(1)}, u32[]{:S(2)}, u32[]{:S(2)}) %all-to-all-start.3) | async-done | bytes 131104 | tf_op jit(solution)/shard_map/all_to_all | solution.py:32
  107.6 4.4 %all-to-all-start.1 = ((f32[64,1,256]{2,1,0:T(1,128)}), f32[64,1,256]{2,1,0:T(1,128)S(1)}, u32[]{:S(2)}, u32[]{:S(2)}) async-start(f32[64,1,256]{2,1,0:T(1,128)} %reshape.168), calls=%async_computation.1 | async-start | bytes 131072 | tf_op jit(solution)/shard_map/all_to_all | solution.py:32
  112.1 1.0 reduce.13
  113.6 0.6 gather_fusion
  114.3 0.6 gather_fusion.1
  114.9 0.6 gather_fusion.2
  116.2 6.0 %all-to-all-done.1 = f32[64,1,256]{2,1,0:T(1,128)S(1)} async-done(((f32[64,1,256]{2,1,0:T(1,128)}), f32[64,1,256]{2,1,0:T(1,128)S(1)}, u32[]{:S(2)}, u32[]{:S(2)}) %all-to-all-start.1) | async-done | bytes 65568 | tf_op jit(solution)/shard_map/all_to_all | solution.py:32
  122.2 0.6 broadcast_in_dim.188
  122.8 4.0 %all-to-all-start.4 = ((f32[4,1,64]{2,1,0:T(1,128)}), f32[4,1,64]{2,1,0:T(1,128)S(1)}, u32[]{:S(2)}, u32[]{:S(2)}) async-start(f32[4,1,64]{2,1,0:T(1,128)} %broadcast_in_dim.188), calls=%async_computation.4 | async-start | bytes 4096 | tf_op jit(solution)/shard_map/all_to_all | solution.py:32
  126.8 0.8 reduce.11
  128.0 2.8 %all-to-all-done.4 = f32[4,1,64]{2,1,0:T(1,128)S(1)} async-done(((f32[4,1,64]{2,1,0:T(1,128)}), f32[4,1,64]{2,1,0:T(1,128)S(1)}, u32[]{:S(2)}, u32[]{:S(2)}) %all-to-all-start.4) | async-done | bytes 1056 | tf_op jit(solution)/shard_map/all_to_all | solution.py:32
  131.4 0.6 fusion.35
  132.0 1.3 broadcast_in_dim.194
  133.3 5.8 %all-to-all-start.5 = ((f32[64,1,1]{2,1,0:T(1,128)}), f32[64,1,1]{2,1,0:T(1,128)S(1)}, u32[]{:S(2)}, u32[]{:S(2)}) async-start(f32[64,1,1]{2,1,0:T(1,128)} %broadcast_in_dim.194), calls=%async_computation.5 | async-start | bytes 65536 | tf_op jit(solution)/shard_map/all_to_all | solution.py:32
  139.3 0.8 copy.62
  140.1 8.5 %all-to-all-done.5 = f32[64,1,1]{2,1,0:T(1,128)S(1)} async-done(((f32[64,1,1]{2,1,0:T(1,128)}), f32[64,1,1]{2,1,0:T(1,128)S(1)}, u32[]{:S(2)}, u32[]{:S(2)}) %all-to-all-start.5) | async-done | bytes 288 | tf_op jit(solution)/shard_map/all_to_all | solution.py:32
  148.6 0.7 reduce_sum.165
  150.0 0.7 broadcast_multiply_fusion
  (187 shorter events, 8.1 us)
Async XLA Ops:
  26.6 14.5 %copy-start.9 = (s32[16]{0:T(128)S(1)}, s32[16]{0:T(128)}, u32[]{:S(2)}) copy-start(s32[16]{0:T(128)} %param.20) | copy-start | bytes 196
  26.6 14.5 %copy-start.4 = (s32[15360]{0:T(1024)S(1)}, s32[15360]{0:T(1024)}, u32[]{:S(2)}) copy-start(s32[15360]{0:T(1024)} %param.14) | copy-start | bytes 184324
  26.6 14.5 %copy-start.7 = (s32[8]{0:T(128)S(1)}, s32[8]{0:T(128)}, u32[]{:S(2)}) copy-start(s32[8]{0:T(128)} %param.19) | copy-start | bytes 100
  26.6 14.5 %copy-start.8 = (s32[8]{0:T(128)S(1)}, s32[8]{0:T(128)}, u32[]{:S(2)}) copy-start(s32[8]{0:T(128)} %param.18) | copy-start | bytes 100
  26.6 15.0 %copy-start = (s32[16,15360]{1,0:T(8,128)S(1)}, s32[16,15360]{1,0:T(8,128)}, u32[]{:S(2)}) copy-start(s32[16,15360]{1,0:T(8,128)} %param.13) | copy-start | bytes 2949124
  27.8 14.1 %copy-start.6 = (s32[16]{0:T(128)S(1)}, s32[16]{0:T(128)}, u32[]{:S(2)}) copy-start(s32[16]{0:T(128)} %param.21) | copy-start | bytes 196
  27.8 40.2 %all-to-all-start = ((f32[64,1,256]{2,1,0:T(1,128)}), f32[64,1,256]{2,1,0:T(1,128)S(1)}, u32[]{:S(2)}, u32[]{:S(2)}) async-start(f32[64,1,256]{2,1,0:T(1,128)} %reshape.166), calls=%async_computation | async-start | bytes 131072 | tf_op jit(solution)/shard_map/all_to_all | solution.py:20
  68.0 21.4 %all-to-all-start.2 = ((f32[64,1,512]{2,1,0:T(1,128)}), f32[64,1,512]{2,1,0:T(1,128)S(1)}, u32[]{:S(2)}, u32[]{:S(2)}) async-start(f32[64,1,512]{2,1,0:T(1,128)} %reshape.170), calls=%async_computation.2 | async-start | bytes 262144 | tf_op jit(solution)/shard_map/all_to_all | solution.py:20
  91.9 15.8 %all-to-all-start.3 = ((f32[64,1,512]{2,1,0:T(1,128)}), f32[64,1,512]{2,1,0:T(1,128)S(1)}, u32[]{:S(2)}, u32[]{:S(2)}) async-start(f32[64,1,512]{2,1,0:T(1,128)} %reshape.172), calls=%async_computation.3 | async-start | bytes 262144 | tf_op jit(solution)/shard_map/all_to_all | solution.py:32
  107.6 14.6 %all-to-all-start.1 = ((f32[64,1,256]{2,1,0:T(1,128)}), f32[64,1,256]{2,1,0:T(1,128)S(1)}, u32[]{:S(2)}, u32[]{:S(2)}) async-start(f32[64,1,256]{2,1,0:T(1,128)} %reshape.168), calls=%async_computation.1 | async-start | bytes 131072 | tf_op jit(solution)/shard_map/all_to_all | solution.py:32
  113.6 14.4 %copy-start.1 = (f32[4,32,256]{2,1,0:T(8,128)}, f32[4,32,256]{2,1,0:T(8,128)S(1)}, u32[]{:S(2)}) copy-start(f32[4,32,256]{2,1,0:T(8,128)S(1)} %copy.63) | copy-start | bytes 393220
  114.2 17.2 %copy-start.2 = (f32[15360]{0:T(1024)S(1)}, f32[15360]{0:T(1024)}, u32[]{:S(2)}) copy-start(f32[15360]{0:T(1024)} %param.16) | copy-start | bytes 184324
  114.2 17.2 %copy-start.3 = (f32[15360]{0:T(1024)S(1)}, f32[15360]{0:T(1024)}, u32[]{:S(2)}) copy-start(f32[15360]{0:T(1024)} %param.15) | copy-start | bytes 184324
  122.8 8.1 %all-to-all-start.4 = ((f32[4,1,64]{2,1,0:T(1,128)}), f32[4,1,64]{2,1,0:T(1,128)S(1)}, u32[]{:S(2)}, u32[]{:S(2)}) async-start(f32[4,1,64]{2,1,0:T(1,128)} %broadcast_in_dim.188), calls=%async_computation.4 | async-start | bytes 4096 | tf_op jit(solution)/shard_map/all_to_all | solution.py:32
  130.9 8.4 %copy-start.10 = (f32[32]{0:T(128)}, f32[32]{0:T(128)S(1)}, u32[]{:S(2)}) copy-start(f32[32]{0:T(128)S(1)} %add_divide_fusion) | copy-start | bytes 388
  133.3 15.3 %all-to-all-start.5 = ((f32[64,1,1]{2,1,0:T(1,128)}), f32[64,1,1]{2,1,0:T(1,128)S(1)}, u32[]{:S(2)}, u32[]{:S(2)}) async-start(f32[64,1,1]{2,1,0:T(1,128)} %broadcast_in_dim.194), calls=%async_computation.5 | async-start | bytes 65536 | tf_op jit(solution)/shard_map/all_to_all | solution.py:32
  139.2 10.8 %copy-start.5 = (f32[15360]{0:T(1024)S(1)}, f32[15360]{0:T(1024)}, u32[]{:S(2)}) copy-start(f32[15360]{0:T(1024)} %param.17) | copy-start | bytes 184324
where the time goes:
time: 151 us
  matrix products  43.1 us (29%)
  starting transfers between devices  42.3 us (28%)
  waiting for transfers between devices  36.7 us (24%)
  local copies, waits for them, and re-layouts  16.2 us (11%)
  other arithmetic  9.37 us (6%)
  between operations  1.8 us (1%)
    dot_general x30, matrix products, accumulate(): jnp.einsum('rn,frb->fnb', row_matrix, onehot_bins, preferred_element_type...  43.1 us
    all_to_all x4, waiting for transfers between devices, copy_for_each(): lax.all_to_all(jnp.broadcast_to(shard[None], (length, *shard.shape)), axi...  27.4 us
    all_to_all x2, starting transfers between devices, summed_on_arrival(): lax.all_to_all(in_blocks(shard, dim, length), axis, 0, 0, tiled=True)  23.6 us
    all_to_all x4, starting transfers between devices, copy_for_each(): lax.all_to_all(jnp.broadcast_to(shard[None], (length, *shard.shape)), axi...  18.8 us
    all_to_all x2, waiting for transfers between devices, summed_on_arrival(): lax.all_to_all(in_blocks(shard, dim, length), axis, 0, 0, tiled=True)  9.36 us
    unnamed x34, local copies, waits for them, and re-layouts  6.57 us
  transfers between devices with their start and end apart: 6, of which 5 were waited for; matrix products, arithmetic and copies ran while one was open for 23% of the time, Pallas kernels for 0%

commit v1 on v0

v1 whole, which is shorter than its diff:
```python
import functools

import jax
import jax.numpy as jnp
from jax import lax
from jax.experimental import pallas as pl
from jax.experimental.pallas import tpu as pltpu
from jax.sharding import PartitionSpec as P

FEATURES = 16
BINS = 256
NODES3 = 8
NODES4 = 16
LEAVES = 32
LANES = 128
GROUP = 8
MESH = pl.DeviceIdType.MESH
F32 = jnp.float32
BF16 = jnp.bfloat16


def flipped(index, mask):
    out = index
    for bit in (1, 2, 4):
        if mask & bit:
            out = out + bit * (1 - 2 * ((index // bit) % 2))
    return out


def tree_sum(parts):
    while len(parts) > 1:
        parts = [a + b for a, b in zip(parts[::2], parts[1::2])]
    return parts[0]


def kernel(
    total_rows,
    own_features,
    f3_ref,
    b3_ref,
    f4_ref,
    b4_ref,
    codes_ref,
    node_ref,
    label_ref,
    weight_ref,
    pred_ref,
    hist3_ref,
    hist4_ref,
    leaf_value_ref,
    new_pred_ref,
    new_weight_ref,
    key_ref,
    low_ref,
    wr_ref,
    sr_ref,
    leaf_ref,
    leafrow_ref,
    stat_ref,
    acc_ref,
    rs_ref,
    mid_ref,
    ar_ref,
    tot_ref,
    leaf_a_ref,
    leaf_b_ref,
    leaf_mid_ref,
    send_sem,
    rs_sem,
    ar_sem,
    ag_sem,
    leaf_send_sem,
    leaf_sem,
):
    tiles = node_ref.shape[0]
    steps = tiles // 8
    row = lax.axis_index("rows")
    feat = lax.axis_index("feat")
    group = row % GROUP
    plane = row // GROUP
    in_group = [(plane * GROUP + flipped(group, j), feat) for j in range(1, GROUP)]
    in_line = [(flipped(plane, j) * GROUP + group, feat) for j in range(1, GROUP)]

    barrier = pltpu.get_barrier_semaphore()
    for peer in in_group + in_line:
        pl.semaphore_signal(barrier, inc=1, device_id=peer, device_id_type=MESH)

    features3 = [f3_ref[i] for i in range(NODES3)]
    bins3 = [b3_ref[i] for i in range(NODES3)]
    features4 = [f4_ref[i] for i in range(NODES4)]
    bins4 = [b4_ref[i] for i in range(NODES4)]

    def lookup(where_of, tables):
        outs = [jnp.full((8, LANES), table[0], jnp.int32) for table in tables]
        for i in range(1, len(tables[0])):
            hit = where_of == i
            outs = [jnp.where(hit, table[i], out) for table, out in zip(tables, outs)]
        return outs

    def route(step, carry):
        rows = pl.ds(step * 8, 8)
        node = node_ref[rows, :]
        codes = [
            codes_ref[pl.ds((f // 8) * tiles * 8 + step * 64 + f % 8, 8, stride=8), :]
            for f in range(FEATURES)
        ]

        def side(node_of, features, bins):
            chosen, cutoff = lookup(node_of, [features, bins])
            picked = codes[0]
            for f in range(1, FEATURES):
                picked = jnp.where(chosen == f, codes[f], picked)
            return 2 * node_of + jnp.where(picked > cutoff, 1, 0)

        node4 = side(node, features3, bins3)
        leaf = side(node4, features4, bins4)
        leaf_ref[rows, :] = leaf
        leafrow_ref[rows, :] = leaf.astype(F32)
        for f in range(own_features):
            index = feat * own_features + f
            start = (index // 8) * (tiles * 8) + step * 64 + index % 8
            code = codes_ref[pl.ds(start, 8, stride=8), :]
            low_ref[f, rows, :] = (code & (LANES - 1)).astype(F32)
            key_ref[f, rows, :] = (node4 + NODES4 * (code >> 7)).astype(F32)
        weight = weight_ref[rows, :]
        label = label_ref[rows, :]
        rounded = weight.astype(BF16).astype(F32)
        wr_ref[rows, :] = rounded
        sr_ref[rows, :] = (weight * label).astype(BF16).astype(F32)
        rest = weight - rounded
        middle = rest.astype(BF16).astype(F32)
        low = rest - middle
        positive = label > 0.0
        for j, part in enumerate((rounded, middle, low)):
            stat_ref[pl.ds(step * 64 + j, 8, stride=8), :] = jnp.where(positive, part, 0.0)
            stat_ref[pl.ds(step * 64 + 3 + j, 8, stride=8), :] = jnp.where(positive, 0.0, part)
        for j in (6, 7):
            stat_ref[pl.ds(step * 64 + j, 8, stride=8), :] = jnp.zeros((8, LANES), F32)
        return carry

    lax.fori_loop(0, steps, route, 0)

    sub = lax.broadcasted_iota(jnp.int32, (16, LANES), 0).astype(F32)
    zero = jnp.zeros((16, LANES), BF16)
    one = jnp.ones((16, LANES), BF16)
    numbers = [(sub + 16 * i).astype(BF16) for i in range(8)]

    def spread(ref, *index):
        return jnp.broadcast_to(ref[index], (16, LANES)).astype(BF16)

    def dot_nt(a, b):
        return lax.dot_general(a, b, (((1,), (1,)), ((), ())), preferred_element_type=F32)

    def leaf_step(step, acc):
        left, right = [], []
        for i in range(8):
            t = step * 8 + i
            left.append(stat_ref[pl.ds(t * 8, 8), :].astype(BF16))
            at = spread(leafrow_ref, pl.ds(t, 1), slice(None))
            right.append(
                jnp.concatenate([jnp.where(at == numbers[k], one, zero) for k in range(2)], axis=0)
            )
        return acc + dot_nt(jnp.concatenate(left, axis=1), jnp.concatenate(right, axis=1))

    leaf_sums = lax.fori_loop(0, steps, leaf_step, jnp.zeros((8, LEAVES), F32))
    leaf_a_ref[0, :, :] = jnp.zeros((8, LANES), F32)
    leaf_a_ref[0, :, :LEAVES] = leaf_sums

    pl.semaphore_wait(barrier, 2 * (GROUP - 1))

    sends = []

    def send(source, target, sem, recv, peer):
        copy = pltpu.make_async_remote_copy(
            src_ref=source, dst_ref=target, send_sem=sem, recv_sem=recv, device_id=peer, device_id_type=MESH
        )
        copy.start()
        sends.append(copy)

    def arrived(ref, sem):
        pltpu.make_async_copy(ref, ref, sem).wait()

    for j in range(1, GROUP):
        send(leaf_a_ref.at[0], leaf_a_ref.at[j], leaf_send_sem.at[0, j - 1], leaf_sem.at[0], in_group[j - 1])

    def hist_step(f, step, acc):
        left, right = [], []
        for i in range(8):
            t = step * 8 + i
            key = spread(key_ref, f, pl.ds(t, 1), slice(None))
            low = spread(low_ref, f, pl.ds(t, 1), slice(None))
            wr = spread(wr_ref, pl.ds(t, 1), slice(None))
            sr = spread(sr_ref, pl.ds(t, 1), slice(None))
            blocks = []
            for hi in range(2):
                hit = key == numbers[hi]
                blocks += [jnp.where(hit, wr, zero), jnp.where(hit, sr, zero)]
            left.append(jnp.concatenate(blocks, axis=0))
            right.append(
                jnp.concatenate([jnp.where(low == numbers[k], one, zero) for k in range(8)], axis=0)
            )
        return acc + dot_nt(jnp.concatenate(left, axis=1), jnp.concatenate(right, axis=1))

    def compute(f):
        acc_ref[f, :, :] = lax.fori_loop(
            0, steps, functools.partial(hist_step, f), jnp.zeros((64, LANES), F32)
        )
        rs_ref[f, 0, :, :] = acc_ref[f, pl.ds(pl.multiple_of(group * 8, 8), 8), :]

    def scatter(f):
        for j in range(1, GROUP):
            rows = pl.ds(pl.multiple_of(flipped(group, j) * 8, 8), 8)
            send(acc_ref.at[f, rows], rs_ref.at[f, j], send_sem.at[f, 0, j - 1], rs_sem.at[f], in_group[j - 1])

    def exchange(f):
        arrived(rs_ref.at[f, pl.ds(1, GROUP - 1)], rs_sem.at[f])
        ar_ref[f, 0, :, :] = tree_sum([rs_ref[f, j] for j in range(GROUP)])
        for j in range(1, GROUP):
            send(ar_ref.at[f, 0], ar_ref.at[f, j], send_sem.at[f, 1, j - 1], ar_sem.at[f], in_line[j - 1])

    def gather(f):
        arrived(ar_ref.at[f, pl.ds(1, GROUP - 1)], ar_sem.at[f])
        mid_ref[f, :, :] = tree_sum([ar_ref[f, j] for j in range(GROUP)])
        rows = pl.ds(pl.multiple_of(group * 8, 8), 8)
        tot_ref[f, rows, :] = mid_ref[f, :, :]
        for j in range(1, GROUP):
            send(mid_ref.at[f], tot_ref.at[f, rows], send_sem.at[f, 2, j - 1], ag_sem.at[f], in_group[j - 1])

    compute(0)
    scatter(0)
    compute(1)
    scatter(1)

    arrived(leaf_a_ref.at[pl.ds(1, GROUP - 1)], leaf_sem.at[0])
    leaf_b_ref[0, :, :] = tree_sum([leaf_a_ref[j] for j in range(GROUP)])
    for j in range(1, GROUP):
        send(leaf_b_ref.at[0], leaf_b_ref.at[j], leaf_send_sem.at[1, j - 1], leaf_sem.at[1], in_line[j - 1])

    compute(2)
    scatter(2)
    exchange(0)
    compute(3)
    scatter(3)
    exchange(1)
    exchange(2)

    arrived(leaf_b_ref.at[pl.ds(1, GROUP - 1)], leaf_sem.at[1])
    leaf_mid_ref[...] = tree_sum([leaf_b_ref[j] for j in range(GROUP)])
    plus = leaf_mid_ref[0:1, :]
    minus = leaf_mid_ref[3:4, :]
    values = (plus - minus) / ((plus + minus) + 1.0)
    leaf_value_ref[...] = values
    all_plus = plus + (leaf_mid_ref[1:2, :] + leaf_mid_ref[2:3, :])
    all_minus = minus + (leaf_mid_ref[4:5, :] + leaf_mid_ref[5:6, :])
    grand = jnp.sum(all_plus * jnp.exp(-values) + all_minus * jnp.exp(values), axis=1, keepdims=True)
    scale = jnp.broadcast_to(total_rows / grand, (8, LANES))
    table = jnp.broadcast_to(values, (8, LANES))

    def update(step, carry):
        rows = pl.ds(step * 8, 8)
        stepped = jnp.take_along_axis(table, leaf_ref[rows, :], axis=1)
        new_pred_ref[rows, :] = pred_ref[rows, :] + stepped
        raw = weight_ref[rows, :] * jnp.exp(-label_ref[rows, :] * stepped)
        new_weight_ref[rows, :] = raw * scale
        return carry

    lax.fori_loop(0, steps, update, 0)

    exchange(3)
    for f in range(own_features):
        gather(f)
    for f in range(own_features):
        arrived(tot_ref.at[f, pl.ds(0, 8 * (GROUP - 1))], ag_sem.at[f])
        for hi in range(2):
            lanes = slice(hi * LANES, (hi + 1) * LANES)
            base = hi * 2 * NODES4
            hist4_ref[f, :, lanes] = tot_ref[f, base : base + 2 * NODES4, :]
            even = tot_ref[f, pl.ds(base, 2 * NODES3, stride=2), :]
            odd = tot_ref[f, pl.ds(base + 1, 2 * NODES3, stride=2), :]
            hist3_ref[f, :, lanes] = even + odd
    for copy in sends:
        copy.wait_send()


def on_device(bin_codes, node_ids, labels, weights, predictions, f3, b3, f4, b4):
    rows = node_ids.shape[0]
    tiles = rows // LANES
    total_rows = float(rows * lax.axis_size("rows"))
    own = FEATURES // lax.axis_size("feat")
    codes = bin_codes.reshape(FEATURES // 8, 8, tiles, LANES).transpose(0, 2, 1, 3)
    codes = codes.reshape(FEATURES * tiles, LANES)
    dense = [a.reshape(tiles, LANES) for a in (node_ids, labels, weights, predictions)]
    smem = pl.BlockSpec(memory_space=pltpu.SMEM)
    vmem = pl.BlockSpec(memory_space=pltpu.VMEM)
    outs = pl.pallas_call(
        functools.partial(kernel, total_rows, own),
        name="grow",
        in_specs=[smem] * 4 + [vmem] * 5,
        out_specs=[vmem] * 5,
        out_shape=[
            jax.ShapeDtypeStruct((own, 2 * NODES3, BINS), F32),
            jax.ShapeDtypeStruct((own, 2 * NODES4, BINS), F32),
            jax.ShapeDtypeStruct((1, LANES), F32),
            jax.ShapeDtypeStruct((tiles, LANES), F32),
            jax.ShapeDtypeStruct((tiles, LANES), F32),
        ],
        scratch_shapes=[
            pltpu.VMEM((own, tiles, LANES), F32),
            pltpu.VMEM((own, tiles, LANES), F32),
            pltpu.VMEM((tiles, LANES), F32),
            pltpu.VMEM((tiles, LANES), F32),
            pltpu.VMEM((tiles, LANES), jnp.int32),
            pltpu.VMEM((tiles, LANES), F32),
            pltpu.VMEM((tiles * 8, LANES), F32),
            pltpu.VMEM((own, 64, LANES), F32),
            pltpu.VMEM((own, GROUP, 8, LANES), F32),
            pltpu.VMEM((own, 8, LANES), F32),
            pltpu.VMEM((own, GROUP, 8, LANES), F32),
            pltpu.VMEM((own, 64, LANES), F32),
            pltpu.VMEM((GROUP, 8, LANES), F32),
            pltpu.VMEM((GROUP, 8, LANES), F32),
            pltpu.VMEM((8, LANES), F32),
            pltpu.SemaphoreType.DMA((own, 3, GROUP - 1)),
            pltpu.SemaphoreType.DMA((own,)),
            pltpu.SemaphoreType.DMA((own,)),
            pltpu.SemaphoreType.DMA((own,)),
            pltpu.SemaphoreType.DMA((2, GROUP - 1)),
            pltpu.SemaphoreType.DMA((2,)),
        ],
        compiler_params=pltpu.CompilerParams(collective_id=0, has_side_effects=True),
    )(f3, b3, f4, b4, codes, *dense)
    hist3, hist4, leaf_values, new_pred, new_weight = outs
    return (
        hist3,
        hist4,
        leaf_values[0, :LEAVES],
        new_pred.reshape(rows),
        new_weight.reshape(rows),
    )


def solution(mesh):
    placed = (P(None, "rows"), P("rows"), P("rows"), P("rows"), P("rows"), P(), P(), P(), P())
    return jax.shard_map(
        on_device,
        mesh=mesh,
        in_specs=placed,
        out_specs=(P("feat", None, None), P("feat", None, None), P(), P("rows"), P("rows")),
        check_vma=False,
    )
```

time: 151 us -> 43.1 us (0.29)
  matrix products: 43.1 us -> 0 us
  starting transfers between devices: 42.3 us -> 0 us
  Pallas kernels: 0 us -> 37.2 us
  waiting for transfers between devices: 36.7 us -> 0 us
  local copies, waits for them, and re-layouts: 16.2 us -> 5.02 us
  other arithmetic: 9.37 us -> 0 us
    dot_general x30 -> x0, matrix products: 43.1 us -> none  [accumulate(): jnp.einsum('rn,frb->fnb', row_matrix, onehot_bins, preferred_element_type...]
    all_to_all x6 -> x0, starting transfers between devices: 42.3 us -> none  [the longest x2 23.6 us: summed_on_arrival(): lax.all_to_all(in_blocks(shard, dim, length), axis, 0, 0, tiled=True)]
    pallas_call x0 -> x1, Pallas kernels: none -> 37.2 us  [on_device(): pl.pallas_call(functools.partial(kernel, total_rows, own), name='grow', i...]
    all_to_all x6 -> x0, waiting for transfers between devices: 36.7 us -> none  [the longest x4 27.4 us: copy_for_each(): lax.all_to_all(jnp.broadcast_to(shard[None], (length, *shard.shape)), axi...]
    reduce_sum x11 -> x0, other arithmetic: 3.6 us -> none  [the longest x2 0.91 us: routing(): cutoff = jnp.sum(jnp.where(member, thresholds[None, :], 0), axis=1)]
    all_to_all x4 -> x0, other arithmetic: 3.51 us -> none  [the longest x2 1.76 us: copy_for_each(): lax.all_to_all(jnp.broadcast_to(shard[None], (length, *shard.shape)), axi...]
    dynamic_slice x61 -> x0, local copies, waits for them, and re-layouts: 2.95 us -> none  [the longest x60 1.86 us: partial_histogram(): lax.scan(accumulate, initial, (code_blocks, node_blocks, weight_blocks, s...]
    unnamed x34 -> x10, local copies, waits for them, and re-layouts: 6.57 us -> 3.81 us
  transfers between devices with their start and end apart: 6 -> 0, of which waited for: 5 -> 0; matrix products, arithmetic and copies ran while one was open for 23% -> 0% of each run, Pallas kernels for 0% -> 0%
where the time goes in v1:
time: 43.1 us; the launch traced here: 42.8 us
  Pallas kernels  37.2 us (86%)
  local copies, waits for them, and re-layouts  5.02 us (12%)
  between operations  0.66 us (2%)
    pallas_call x1, Pallas kernels, on_device(): pl.pallas_call(functools.partial(kernel, total_rows, own), name='grow', i...  37.2 us
    unnamed x10, local copies, waits for them, and re-layouts  3.81 us
    squeeze x1, local copies, waits for them, and re-layouts, on_device(): leaf_values[0, :LEAVES]  1.21 us

profile of v1, /device:TPU:1, one launch (start us, length us, event | category | flops | bytes accessed | tf_op | source)
XLA Modules:
  0.0 42.8 jit_solution(711986172630132223)
XLA Ops:
  0.6 37.2 %grow.1 = (f32[4,16,256]{2,1,0:T(8,128)}, f32[4,32,256]{2,1,0:T(8,128)}, f32[1,128]{1,0:T(1,128)}, f32[120,128]{1,0:T(8,128)}, f32[120,128]{1,0:T(8,128)}) custom-call(s32[8]{0:T(128)} %f3_ref.1, s32[8]{0:T(128)} %b3_ref.1, s32[16]{0:T(128)} %f4_ref.1, s32[16]{0:T(128)} %b4_ref.1, s32[1920,128]{1,0:T(8,128)} %bitcast.13, s32[120,128]{1,0:T(8,128)} %bitcast.14, ...), custom_call_target="tpu_custom_call" | custom-call | tf_op jit(solution)/shard_map/grow/pallas_call | solution.py:295
  37.8 0.0 copy-start
  37.8 1.2 %slice_bitcast_fusion = f32[32]{0:T(128)} fusion(f32[1,128]{1,0:T(1,128)} %get-tuple-element.12), kind=kLoop, calls=%fused_computation | loop fusion | bytes 256 | tf_op jit(solution)/shard_map/squeeze | solution.py:336
  39.0 1.5 %copy.18 = f32[4,16,256]{2,1,0:T(8,128)} copy(f32[4,16,256]{2,1,0:T(8,128)} %get-tuple-element.20) | data formatting | bytes 131072
  40.5 0.0 copy-done
  40.5 0.0 copy-start.2
  40.5 0.7 %copy.19 = f32[4,32,256]{2,1,0:T(8,128)} copy(f32[4,32,256]{2,1,0:T(8,128)S(1)} %copy-done) | data formatting | bytes 262144
  41.2 0.2 copy-done.2
  41.4 0.0 copy-start.1
  41.4 0.6 %copy.20 = f32[15360]{0:T(1024)} copy(f32[15360]{0:T(1024)S(1)} %bitcast.19) | data formatting | bytes 122880
  42.0 0.2 copy-done.1
  42.2 0.6 %copy.21 = f32[15360]{0:T(1024)} copy(f32[15360]{0:T(1024)S(1)} %bitcast.18) | data formatting | bytes 122880
Async XLA Ops:
  37.8 2.7 %copy-start = (f32[4,32,256]{2,1,0:T(8,128)S(1)}, f32[4,32,256]{2,1,0:T(8,128)}, u32[]{:S(2)}) copy-start(f32[4,32,256]{2,1,0:T(8,128)} %get-tuple-element.21) | copy-start | bytes 393220
  40.5 0.9 %copy-start.2 = (f32[120,128]{1,0:T(8,128)S(1)}, f32[120,128]{1,0:T(8,128)}, u32[]{:S(2)}) copy-start(f32[120,128]{1,0:T(8,128)} %get-tuple-element.13) | copy-start | bytes 184324
  41.4 0.9 %copy-start.1 = (f32[120,128]{1,0:T(8,128)S(1)}, f32[120,128]{1,0:T(8,128)}, u32[]{:S(2)}) copy-start(f32[120,128]{1,0:T(8,128)} %get-tuple-element.14) | copy-start | bytes 184324

commit v2 on v1

--- a/solution.py
+++ b/solution.py
@@ -13,6 +13,7 @@
 NODES4 = 16
 LEAVES = 32
 LANES = 128
+CHUNKS = 3
 GROUP = 8
 MESH = pl.DeviceIdType.MESH
 F32 = jnp.float32
@@ -36,6 +37,20 @@
 def kernel(
     total_rows,
     own_features,
+    f3_hbm,
+    b3_hbm,
+    f4_hbm,
+    b4_hbm,
+    codes_hbm,
+    node_hbm,
+    label_hbm,
+    weight_hbm,
+    pred_hbm,
+    hist3_ref,
+    hist4_ref,
+    leaf_value_ref,
+    new_pred_ref,
+    new_weight_ref,
     f3_ref,
     b3_ref,
     f4_ref,
@@ -45,11 +60,6 @@
     label_ref,
     weight_ref,
     pred_ref,
-    hist3_ref,
-    hist4_ref,
-    leaf_value_ref,
-    new_pred_ref,
-    new_weight_ref,
     key_ref,
     low_ref,
     wr_ref,
@@ -71,8 +81,10 @@
     ag_sem,
     leaf_send_sem,
     leaf_sem,
+    in_sem,
+    code_sem,
 ):
-    tiles = node_ref.shape[0]
+    tiles = node_hbm.shape[0]
     steps = tiles // 8
     row = lax.axis_index("rows")
     feat = lax.axis_index("feat")
@@ -82,8 +94,36 @@
     in_line = [(flipped(plane, j) * GROUP + group, feat) for j in range(1, GROUP)]
 
     barrier = pltpu.get_barrier_semaphore()
-    for peer in in_group + in_line:
-        pl.semaphore_signal(barrier, inc=1, device_id=peer, device_id_type=MESH)
+    with jax.named_scope('signal'):
+        for peer in in_group + in_line:
+            pl.semaphore_signal(barrier, inc=1, device_id=peer, device_id_type=MESH)
+
+    def fetch(source, target, sem):
+        copy = pltpu.make_async_copy(source, target, sem)
+        copy.start()
+        return copy
+
+    part = tiles * 8 // CHUNKS
+    pieces = [pl.ds(c * part, part) for c in range(CHUNKS)]
+    small = [
+        (f3_hbm, f3_ref),
+        (b3_hbm, b3_ref),
+        (f4_hbm, f4_ref),
+        (b4_hbm, b4_ref),
+        (node_hbm, node_ref),
+        (label_hbm, label_ref),
+        (weight_hbm, weight_ref),
+        (pred_hbm, pred_ref),
+    ]
+    ready = [fetch(a, b, in_sem.at[i]) for i, (a, b) in enumerate(small[:5])]
+    code_ready = []
+    for c in range(CHUNKS):
+        code_ready.append(fetch(codes_hbm.at[:, pieces[c]], codes_ref.at[:, pieces[c]], code_sem.at[c]))
+        if c == 0:
+            ready += [fetch(a, b, in_sem.at[5 + i]) for i, (a, b) in enumerate(small[5:])]
+    with jax.named_scope('inwait'):
+        for copy in ready:
+            copy.wait()
 
     features3 = [f3_ref[i] for i in range(NODES3)]
     bins3 = [b3_ref[i] for i in range(NODES3)]
@@ -101,7 +141,7 @@
         rows = pl.ds(step * 8, 8)
         node = node_ref[rows, :]
         codes = [
-            codes_ref[pl.ds((f // 8) * tiles * 8 + step * 64 + f % 8, 8, stride=8), :]
+            codes_ref[f // 8, pl.ds(step * 64 + f % 8, 8, stride=8), :]
             for f in range(FEATURES)
         ]
 
@@ -118,8 +158,7 @@
         leafrow_ref[rows, :] = leaf.astype(F32)
         for f in range(own_features):
             index = feat * own_features + f
-            start = (index // 8) * (tiles * 8) + step * 64 + index % 8
-            code = codes_ref[pl.ds(start, 8, stride=8), :]
+            code = codes_ref[index // 8, pl.ds(step * 64 + index % 8, 8, stride=8), :]
             low_ref[f, rows, :] = (code & (LANES - 1)).astype(F32)
             key_ref[f, rows, :] = (node4 + NODES4 * (code >> 7)).astype(F32)
         weight = weight_ref[rows, :]
@@ -138,7 +177,10 @@
             stat_ref[pl.ds(step * 64 + j, 8, stride=8), :] = jnp.zeros((8, LANES), F32)
         return carry
 
-    lax.fori_loop(0, steps, route, 0)
+    with jax.named_scope('route'):
+        for c in range(CHUNKS):
+            code_ready[c].wait()
+            lax.fori_loop(c * steps // CHUNKS, (c + 1) * steps // CHUNKS, route, 0, unroll=5)
 
     sub = lax.broadcasted_iota(jnp.int32, (16, LANES), 0).astype(F32)
     zero = jnp.zeros((16, LANES), BF16)
@@ -162,12 +204,6 @@
             )
         return acc + dot_nt(jnp.concatenate(left, axis=1), jnp.concatenate(right, axis=1))
 
-    leaf_sums = lax.fori_loop(0, steps, leaf_step, jnp.zeros((8, LEAVES), F32))
-    leaf_a_ref[0, :, :] = jnp.zeros((8, LANES), F32)
-    leaf_a_ref[0, :, :LEAVES] = leaf_sums
-
-    pl.semaphore_wait(barrier, 2 * (GROUP - 1))
-
     sends = []
 
     def send(source, target, sem, recv, peer):
@@ -180,8 +216,19 @@
     def arrived(ref, sem):
         pltpu.make_async_copy(ref, ref, sem).wait()
 
-    for j in range(1, GROUP):
-        send(leaf_a_ref.at[0], leaf_a_ref.at[j], leaf_send_sem.at[0, j - 1], leaf_sem.at[0], in_group[j - 1])
+    def leaf_scatter():
+        leaf_sums = lax.fori_loop(0, steps, leaf_step, jnp.zeros((8, LEAVES), F32), unroll=5)
+        leaf_a_ref[0, :, :] = jnp.zeros((8, LANES), F32)
+        leaf_a_ref[0, :, :LEAVES] = leaf_sums
+        for j in range(1, GROUP):
+            send(leaf_a_ref.at[0], leaf_a_ref.at[j], leaf_send_sem.at[0, j - 1], leaf_sem.at[0], in_group[j - 1])
+
+    def leaf_exchange():
+        with jax.named_scope('leafwait1'):
+            arrived(leaf_a_ref.at[pl.ds(1, GROUP - 1)], leaf_sem.at[0])
+        leaf_b_ref[0, :, :] = tree_sum([leaf_a_ref[j] for j in range(GROUP)])
+        for j in range(1, GROUP):
+            send(leaf_b_ref.at[0], leaf_b_ref.at[j], leaf_send_sem.at[1, j - 1], leaf_sem.at[1], in_line[j - 1])
 
     def hist_step(f, step, acc):
         left, right = [], []
@@ -199,12 +246,12 @@
             right.append(
                 jnp.concatenate([jnp.where(low == numbers[k], one, zero) for k in range(8)], axis=0)
             )
-        return acc + dot_nt(jnp.concatenate(left, axis=1), jnp.concatenate(right, axis=1))
+        return acc + dot_nt(jnp.concatenate(right, axis=1), jnp.concatenate(left, axis=1))
 
     def compute(f):
         acc_ref[f, :, :] = lax.fori_loop(
-            0, steps, functools.partial(hist_step, f), jnp.zeros((64, LANES), F32)
-        )
+            0, steps, functools.partial(hist_step, f), jnp.zeros((LANES, 64), F32), unroll=5
+        ).T
         rs_ref[f, 0, :, :] = acc_ref[f, pl.ds(pl.multiple_of(group * 8, 8), 8), :]
 
     def scatter(f):
@@ -226,25 +273,46 @@
         for j in range(1, GROUP):
             send(mid_ref.at[f], tot_ref.at[f, rows], send_sem.at[f, 2, j - 1], ag_sem.at[f], in_group[j - 1])
 
-    compute(0)
-    scatter(0)
-    compute(1)
-    scatter(1)
-
-    arrived(leaf_a_ref.at[pl.ds(1, GROUP - 1)], leaf_sem.at[0])
-    leaf_b_ref[0, :, :] = tree_sum([leaf_a_ref[j] for j in range(GROUP)])
-    for j in range(1, GROUP):
-        send(leaf_b_ref.at[0], leaf_b_ref.at[j], leaf_send_sem.at[1, j - 1], leaf_sem.at[1], in_line[j - 1])
-
-    compute(2)
-    scatter(2)
-    exchange(0)
-    compute(3)
-    scatter(3)
-    exchange(1)
-    exchange(2)
-
-    arrived(leaf_b_ref.at[pl.ds(1, GROUP - 1)], leaf_sem.at[1])
+    with jax.named_scope('compute0'):
+        compute(0)
+    with jax.named_scope('compute1'):
+        compute(1)
+    with jax.named_scope('barwait'):
+        pl.semaphore_wait(barrier, 2 * (GROUP - 1))
+    with jax.named_scope('scatter0'):
+        scatter(0)
+    with jax.named_scope('scatter1'):
+        scatter(1)
+    with jax.named_scope('compute2'):
+        compute(2)
+    with jax.named_scope('scatter2'):
+        scatter(2)
+    with jax.named_scope('compute3'):
+        compute(3)
+    with jax.named_scope('scatter3'):
+        scatter(3)
+    with jax.named_scope('exchange0'):
+        exchange(0)
+    with jax.named_scope('exchange1'):
+        exchange(1)
+    with jax.named_scope('leaf_scatter'):
+        leaf_scatter()
+    with jax.named_scope('exchange2'):
+        exchange(2)
+    with jax.named_scope('exchange3'):
+        exchange(3)
+    with jax.named_scope('leaf_exchange'):
+        leaf_exchange()
+    with jax.named_scope('gather0'):
+        gather(0)
+    with jax.named_scope('gather1'):
+        gather(1)
+    with jax.named_scope('gather2'):
+        gather(2)
+    with jax.named_scope('gather3'):
+        gather(3)
+    with jax.named_scope('leafwait2'):
+        arrived(leaf_b_ref.at[pl.ds(1, GROUP - 1)], leaf_sem.at[1])
     leaf_mid_ref[...] = tree_sum([leaf_b_ref[j] for j in range(GROUP)])
     plus = leaf_mid_ref[0:1, :]
     minus = leaf_mid_ref[3:4, :]
@@ -264,13 +332,12 @@
         new_weight_ref[rows, :] = raw * scale
         return carry
 
-    lax.fori_loop(0, steps, update, 0)
-
-    exchange(3)
+    with jax.named_scope('update'):
+        lax.fori_loop(0, steps, update, 0, unroll=5)
+
     for f in range(own_features):
-        gather(f)
-    for f in range(own_features):
-        arrived(tot_ref.at[f, pl.ds(0, 8 * (GROUP - 1))], ag_sem.at[f])
+        with jax.named_scope('agwait'):
+            arrived(tot_ref.at[f, pl.ds(0, 8 * (GROUP - 1))], ag_sem.at[f])
         for hi in range(2):
             lanes = slice(hi * LANES, (hi + 1) * LANES)
             base = hi * 2 * NODES4
@@ -278,8 +345,19 @@
             even = tot_ref[f, pl.ds(base, 2 * NODES3, stride=2), :]
             odd = tot_ref[f, pl.ds(base + 1, 2 * NODES3, stride=2), :]
             hist3_ref[f, :, lanes] = even + odd
-    for copy in sends:
-        copy.wait_send()
+    with jax.named_scope('sendwait'):
+        for copy in sends:
+            copy.wait_send()
+
+
+def store_kernel(h3, h4, values, pred, weight, h3_out, h4_out, values_out, pred_out, weight_out, sem):
+    pairs = [(h3, h3_out), (h4, h4_out), (pred, pred_out), (weight, weight_out)]
+    copies = [pltpu.make_async_copy(a, b, sem.at[i]) for i, (a, b) in enumerate(pairs)]
+    for copy in copies:
+        copy.start()
+    values_out[...] = values[0, :LEAVES]
+    for copy in copies:
+        copy.wait()
 
 
 def on_device(bin_codes, node_ids, labels, weights, predictions, f3, b3, f4, b4):
@@ -288,14 +366,14 @@
     total_rows = float(rows * lax.axis_size("rows"))
     own = FEATURES // lax.axis_size("feat")
     codes = bin_codes.reshape(FEATURES // 8, 8, tiles, LANES).transpose(0, 2, 1, 3)
-    codes = codes.reshape(FEATURES * tiles, LANES)
+    codes = codes.reshape(FEATURES // 8, tiles * 8, LANES)
     dense = [a.reshape(tiles, LANES) for a in (node_ids, labels, weights, predictions)]
-    smem = pl.BlockSpec(memory_space=pltpu.SMEM)
+    held = pl.BlockSpec(memory_space=pltpu.HBM)
     vmem = pl.BlockSpec(memory_space=pltpu.VMEM)
     outs = pl.pallas_call(
         functools.partial(kernel, total_rows, own),
         name="grow",
-        in_specs=[smem] * 4 + [vmem] * 5,
+        in_specs=[held] * 9,
         out_specs=[vmem] * 5,
         out_shape=[
             jax.ShapeDtypeStruct((own, 2 * NODES3, BINS), F32),
@@ -305,6 +383,15 @@
             jax.ShapeDtypeStruct((tiles, LANES), F32),
         ],
         scratch_shapes=[
+            pltpu.SMEM((NODES3,), jnp.int32),
+            pltpu.SMEM((NODES3,), jnp.int32),
+            pltpu.SMEM((NODES4,), jnp.int32),
+            pltpu.SMEM((NODES4,), jnp.int32),
+            pltpu.VMEM(codes.shape, jnp.int32),
+            pltpu.VMEM((tiles, LANES), jnp.int32),
+            pltpu.VMEM((tiles, LANES), F32),
+            pltpu.VMEM((tiles, LANES), F32),
+            pltpu.VMEM((tiles, LANES), F32),
             pltpu.VMEM((own, tiles, LANES), F32),
             pltpu.VMEM((own, tiles, LANES), F32),
             pltpu.VMEM((tiles, LANES), F32),
@@ -326,17 +413,24 @@
             pltpu.SemaphoreType.DMA((own,)),
             pltpu.SemaphoreType.DMA((2, GROUP - 1)),
             pltpu.SemaphoreType.DMA((2,)),
+            pltpu.SemaphoreType.DMA((8,)),
+            pltpu.SemaphoreType.DMA((CHUNKS,)),
         ],
-        compiler_params=pltpu.CompilerParams(collective_id=0, has_side_effects=True),
-    )(f3, b3, f4, b4, codes, *dense)
-    hist3, hist4, leaf_values, new_pred, new_weight = outs
-    return (
-        hist3,
-        hist4,
-        leaf_values[0, :LEAVES],
-        new_pred.reshape(rows),
-        new_weight.reshape(rows),
-    )
+        compiler_params=pltpu.CompilerParams(collective_id=0, has_side_effects=True, vmem_limit_bytes=16 << 20),
+    )(*[pltpu.with_memory_space_constraint(a, pltpu.HBM) for a in (f3, b3, f4, b4, codes, *dense)])
+    hbm = pl.BlockSpec(memory_space=pl.ANY)
+    like = [jax.ShapeDtypeStruct(a.shape, F32) for a in outs]
+    like[2] = jax.ShapeDtypeStruct((LEAVES,), F32)
+    hist3, hist4, leaf_values, new_pred, new_weight = pl.pallas_call(
+        store_kernel,
+        name="store",
+        in_specs=[hbm, hbm, vmem, hbm, hbm],
+        out_specs=[hbm, hbm, vmem, hbm, hbm],
+        out_shape=like,
+        scratch_shapes=[pltpu.SemaphoreType.DMA((4,))],
+        compiler_params=pltpu.CompilerParams(vmem_limit_bytes=1 << 20),
+    )(*outs)
+    return hist3, hist4, leaf_values, new_pred.reshape(rows), new_weight.reshape(rows)
 
 
 def solution(mesh):

time: 43.1 us -> 29.2 us (0.68)
  Pallas kernels: 37.2 us -> 28.5 us
  local copies, waits for them, and re-layouts: 5.02 us -> 0 us
    pallas_call x1, Pallas kernels: 37.2 us -> 27.2 us  [on_device(): pl.pallas_call(functools.partial(kernel, total_rows, own), name='grow', i...]
    unnamed x10 -> x0, local copies, waits for them, and re-layouts: 3.81 us -> none
    pallas_call x0 -> x1, Pallas kernels: none -> 1.26 us  [on_device(): pl.pallas_call(store_kernel, name='store', in_specs=[hbm, hbm, vmem, hbm,...]
    squeeze x1 -> x0, local copies, waits for them, and re-layouts: 1.21 us -> none  [on_device(): leaf_values[0, :LEAVES]]
where the time goes in v2:
time: 29.2 us; the launch traced here: 29.1 us
  Pallas kernels  28.5 us (98%)
  between operations  0.64 us (2%)
    pallas_call x1, Pallas kernels, on_device(): pl.pallas_call(functools.partial(kernel, total_rows, own), name='grow', i...  27.2 us
    pallas_call x1, Pallas kernels, on_device(): pl.pallas_call(store_kernel, name='store', in_specs=[hbm, hbm, vmem, hbm,...  1.26 us

profile of v2, /device:TPU:1, one launch (start us, length us, event | category | flops | bytes accessed | tf_op | source)
XLA Modules:
  0.0 29.1 jit_solution(18164413782871997912)
XLA Ops:
  0.6 27.2 %grow.1 = (f32[4,16,256]{2,1,0:T(8,128)S(1)}, f32[4,32,256]{2,1,0:T(8,128)S(1)}, f32[1,128]{1,0:T(1,128)S(1)}, f32[120,128]{1,0:T(8,128)S(1)}, f32[120,128]{1,0:T(8,128)S(1)}) custom-call(s32[8]{0:T(128)} %f3_hbm.1, s32[8]{0:T(128)} %b3_hbm.1, s32[16]{0:T(128)} %f4_hbm.1, s32[16]{0:T(128)} %b4_hbm.1, s32[2,960,128]{2,1,0:T(8,128)} %bitcast.11, ...), custom_call_target="tpu_custom_call" | custom-call | tf_op jit(solution)/shard_map/grow/pallas_call | solution.py:373
  27.8 1.3 %store.1 = (f32[4,16,256]{2,1,0:T(8,128)}, f32[4,32,256]{2,1,0:T(8,128)}, f32[32]{0:T(128)}, f32[120,128]{1,0:T(8,128)}, f32[120,128]{1,0:T(8,128)}) custom-call(f32[4,16,256]{2,1,0:T(8,128)S(1)} %get-tuple-element.15.h3, f32[4,32,256]{2,1,0:T(8,128)S(1)} %get-tuple-element.16.h4, f32[1,128]{1,0:T(1,128)S(1)} %get-tuple-element.17.values, ...), custom_call_target="tpu_custom_call" | custom-call | tf_op jit(solution)/shard_map/store/pallas_call | solution.py:424

commit v3 on v2

--- a/solution.py
+++ b/solution.py
@@ -116,13 +116,12 @@
         (pred_hbm, pred_ref),
     ]
     ready = [fetch(a, b, in_sem.at[i]) for i, (a, b) in enumerate(small[:5])]
-    code_ready = []
     for c in range(CHUNKS):
-        code_ready.append(fetch(codes_hbm.at[:, pieces[c]], codes_ref.at[:, pieces[c]], code_sem.at[c]))
+        fetch(codes_hbm.at[:, pieces[c]], codes_ref.at[:, pieces[c]], code_sem.at[c])
         if c == 0:
             ready += [fetch(a, b, in_sem.at[5 + i]) for i, (a, b) in enumerate(small[5:])]
-    with jax.named_scope('inwait'):
-        for copy in ready:
+    for i, copy in enumerate(ready):
+        with jax.named_scope('inwait%d' % i):
             copy.wait()
 
     features3 = [f3_ref[i] for i in range(NODES3)]
@@ -177,10 +176,14 @@
             stat_ref[pl.ds(step * 64 + j, 8, stride=8), :] = jnp.zeros((8, LANES), F32)
         return carry
 
+    def route_piece(c, carry):
+        rows = pl.ds(pl.multiple_of(c * part, 8), part)
+        pltpu.make_async_copy(codes_hbm.at[:, rows], codes_ref.at[:, rows], code_sem.at[c]).wait()
+        first = c * (steps // CHUNKS)
+        return lax.fori_loop(0, steps // CHUNKS, lambda i, x: route(first + i, x), carry, unroll=True)
+
     with jax.named_scope('route'):
-        for c in range(CHUNKS):
-            code_ready[c].wait()
-            lax.fori_loop(c * steps // CHUNKS, (c + 1) * steps // CHUNKS, route, 0, unroll=5)
+        lax.fori_loop(0, CHUNKS, route_piece, 0)
 
     sub = lax.broadcasted_iota(jnp.int32, (16, LANES), 0).astype(F32)
     zero = jnp.zeros((16, LANES), BF16)
@@ -204,14 +207,10 @@
             )
         return acc + dot_nt(jnp.concatenate(left, axis=1), jnp.concatenate(right, axis=1))
 
-    sends = []
-
     def send(source, target, sem, recv, peer):
-        copy = pltpu.make_async_remote_copy(
+        pltpu.make_async_remote_copy(
             src_ref=source, dst_ref=target, send_sem=sem, recv_sem=recv, device_id=peer, device_id_type=MESH
-        )
-        copy.start()
-        sends.append(copy)
+        ).start()
 
     def arrived(ref, sem):
         pltpu.make_async_copy(ref, ref, sem).wait()
@@ -221,14 +220,14 @@
         leaf_a_ref[0, :, :] = jnp.zeros((8, LANES), F32)
         leaf_a_ref[0, :, :LEAVES] = leaf_sums
         for j in range(1, GROUP):
-            send(leaf_a_ref.at[0], leaf_a_ref.at[j], leaf_send_sem.at[0, j - 1], leaf_sem.at[0], in_group[j - 1])
+            send(leaf_a_ref.at[0], leaf_a_ref.at[j], leaf_send_sem.at[0], leaf_sem.at[0], in_group[j - 1])
 
     def leaf_exchange():
         with jax.named_scope('leafwait1'):
             arrived(leaf_a_ref.at[pl.ds(1, GROUP - 1)], leaf_sem.at[0])
         leaf_b_ref[0, :, :] = tree_sum([leaf_a_ref[j] for j in range(GROUP)])
         for j in range(1, GROUP):
-            send(leaf_b_ref.at[0], leaf_b_ref.at[j], leaf_send_sem.at[1, j - 1], leaf_sem.at[1], in_line[j - 1])
+            send(leaf_b_ref.at[0], leaf_b_ref.at[j], leaf_send_sem.at[1], leaf_sem.at[1], in_line[j - 1])
 
     def hist_step(f, step, acc):
         left, right = [], []
@@ -250,20 +249,20 @@
 
     def compute(f):
         acc_ref[f, :, :] = lax.fori_loop(
-            0, steps, functools.partial(hist_step, f), jnp.zeros((LANES, 64), F32), unroll=5
+            0, steps, functools.partial(hist_step, f), jnp.zeros((LANES, 64), F32), unroll=15
         ).T
         rs_ref[f, 0, :, :] = acc_ref[f, pl.ds(pl.multiple_of(group * 8, 8), 8), :]
 
     def scatter(f):
         for j in range(1, GROUP):
             rows = pl.ds(pl.multiple_of(flipped(group, j) * 8, 8), 8)
-            send(acc_ref.at[f, rows], rs_ref.at[f, j], send_sem.at[f, 0, j - 1], rs_sem.at[f], in_group[j - 1])
+            send(acc_ref.at[f, rows], rs_ref.at[f, j], send_sem.at[f, 0], rs_sem.at[f], in_group[j - 1])
 
     def exchange(f):
         arrived(rs_ref.at[f, pl.ds(1, GROUP - 1)], rs_sem.at[f])
         ar_ref[f, 0, :, :] = tree_sum([rs_ref[f, j] for j in range(GROUP)])
         for j in range(1, GROUP):
-            send(ar_ref.at[f, 0], ar_ref.at[f, j], send_sem.at[f, 1, j - 1], ar_sem.at[f], in_line[j - 1])
+            send(ar_ref.at[f, 0], ar_ref.at[f, j], send_sem.at[f, 1], ar_sem.at[f], in_line[j - 1])
 
     def gather(f):
         arrived(ar_ref.at[f, pl.ds(1, GROUP - 1)], ar_sem.at[f])
@@ -271,26 +270,25 @@
         rows = pl.ds(pl.multiple_of(group * 8, 8), 8)
         tot_ref[f, rows, :] = mid_ref[f, :, :]
         for j in range(1, GROUP):
-            send(mid_ref.at[f], tot_ref.at[f, rows], send_sem.at[f, 2, j - 1], ag_sem.at[f], in_group[j - 1])
-
-    with jax.named_scope('compute0'):
-        compute(0)
-    with jax.named_scope('compute1'):
-        compute(1)
-    with jax.named_scope('barwait'):
-        pl.semaphore_wait(barrier, 2 * (GROUP - 1))
-    with jax.named_scope('scatter0'):
-        scatter(0)
-    with jax.named_scope('scatter1'):
-        scatter(1)
-    with jax.named_scope('compute2'):
-        compute(2)
-    with jax.named_scope('scatter2'):
-        scatter(2)
-    with jax.named_scope('compute3'):
-        compute(3)
-    with jax.named_scope('scatter3'):
-        scatter(3)
+            send(mid_ref.at[f], tot_ref.at[f, rows], send_sem.at[f, 2], ag_sem.at[f], in_group[j - 1])
+
+    def grow_feature(f, carry):
+        with jax.named_scope('compute'):
+            compute(f)
+
+        @pl.when(f == 1)
+        def _():
+            with jax.named_scope('barwait'):
+                pl.semaphore_wait(barrier, 2 * (GROUP - 1))
+            scatter(0)
+
+        @pl.when(f >= 1)
+        def _():
+            scatter(f)
+
+        return carry
+
+    lax.fori_loop(0, own_features, grow_feature, 0)
     with jax.named_scope('exchange0'):
         exchange(0)
     with jax.named_scope('exchange1'):
@@ -317,7 +315,7 @@
     plus = leaf_mid_ref[0:1, :]
     minus = leaf_mid_ref[3:4, :]
     values = (plus - minus) / ((plus + minus) + 1.0)
-    leaf_value_ref[...] = values
+    leaf_value_ref[...] = values[0, :LEAVES]
     all_plus = plus + (leaf_mid_ref[1:2, :] + leaf_mid_ref[2:3, :])
     all_minus = minus + (leaf_mid_ref[4:5, :] + leaf_mid_ref[5:6, :])
     grand = jnp.sum(all_plus * jnp.exp(-values) + all_minus * jnp.exp(values), axis=1, keepdims=True)
@@ -335,6 +333,13 @@
     with jax.named_scope('update'):
         lax.fori_loop(0, steps, update, 0, unroll=5)
 
+    everything = pl.ds(1, GROUP - 1)
+    with jax.named_scope('sendwait'):
+        for f in range(own_features):
+            arrived(rs_ref.at[f, everything], send_sem.at[f, 0])
+            arrived(ar_ref.at[f, everything], send_sem.at[f, 1])
+        arrived(leaf_a_ref.at[everything], leaf_send_sem.at[0])
+        arrived(leaf_b_ref.at[everything], leaf_send_sem.at[1])
     for f in range(own_features):
         with jax.named_scope('agwait'):
             arrived(tot_ref.at[f, pl.ds(0, 8 * (GROUP - 1))], ag_sem.at[f])
@@ -346,16 +351,16 @@
             odd = tot_ref[f, pl.ds(base + 1, 2 * NODES3, stride=2), :]
             hist3_ref[f, :, lanes] = even + odd
     with jax.named_scope('sendwait'):
-        for copy in sends:
-            copy.wait_send()
-
-
-def store_kernel(h3, h4, values, pred, weight, h3_out, h4_out, values_out, pred_out, weight_out, sem):
-    pairs = [(h3, h3_out), (h4, h4_out), (pred, pred_out), (weight, weight_out)]
-    copies = [pltpu.make_async_copy(a, b, sem.at[i]) for i, (a, b) in enumerate(pairs)]
+        for f in range(own_features):
+            arrived(tot_ref.at[f, pl.ds(0, 8 * (GROUP - 1))], send_sem.at[f, 2])
+
+
+def store_kernel(*refs):
+    count = len(refs) // 2
+    sem = refs[-1]
+    copies = [pltpu.make_async_copy(refs[i], refs[count + i], sem.at[i]) for i in range(count)]
     for copy in copies:
         copy.start()
-    values_out[...] = values[0, :LEAVES]
     for copy in copies:
         copy.wait()
 
@@ -378,7 +383,7 @@
         out_shape=[
             jax.ShapeDtypeStruct((own, 2 * NODES3, BINS), F32),
             jax.ShapeDtypeStruct((own, 2 * NODES4, BINS), F32),
-            jax.ShapeDtypeStruct((1, LANES), F32),
+            jax.ShapeDtypeStruct((LEAVES,), F32),
             jax.ShapeDtypeStruct((tiles, LANES), F32),
             jax.ShapeDtypeStruct((tiles, LANES), F32),
         ],
@@ -407,27 +412,25 @@
             pltpu.VMEM((GROUP, 8, LANES), F32),
             pltpu.VMEM((GROUP, 8, LANES), F32),
             pltpu.VMEM((8, LANES), F32),
-            pltpu.SemaphoreType.DMA((own, 3, GROUP - 1)),
+            pltpu.SemaphoreType.DMA((own, 3)),
             pltpu.SemaphoreType.DMA((own,)),
             pltpu.SemaphoreType.DMA((own,)),
             pltpu.SemaphoreType.DMA((own,)),
-            pltpu.SemaphoreType.DMA((2, GROUP - 1)),
+            pltpu.SemaphoreType.DMA((2,)),
             pltpu.SemaphoreType.DMA((2,)),
             pltpu.SemaphoreType.DMA((8,)),
             pltpu.SemaphoreType.DMA((CHUNKS,)),
         ],
         compiler_params=pltpu.CompilerParams(collective_id=0, has_side_effects=True, vmem_limit_bytes=16 << 20),
     )(*[pltpu.with_memory_space_constraint(a, pltpu.HBM) for a in (f3, b3, f4, b4, codes, *dense)])
-    hbm = pl.BlockSpec(memory_space=pl.ANY)
-    like = [jax.ShapeDtypeStruct(a.shape, F32) for a in outs]
-    like[2] = jax.ShapeDtypeStruct((LEAVES,), F32)
+    anywhere = pl.BlockSpec(memory_space=pl.ANY)
     hist3, hist4, leaf_values, new_pred, new_weight = pl.pallas_call(
         store_kernel,
         name="store",
-        in_specs=[hbm, hbm, vmem, hbm, hbm],
-        out_specs=[hbm, hbm, vmem, hbm, hbm],
-        out_shape=like,
-        scratch_shapes=[pltpu.SemaphoreType.DMA((4,))],
+        in_specs=[anywhere] * len(outs),
+        out_specs=[anywhere] * len(outs),
+        out_shape=[jax.ShapeDtypeStruct(a.shape, F32) for a in outs],
+        scratch_shapes=[pltpu.SemaphoreType.DMA((len(outs),))],
         compiler_params=pltpu.CompilerParams(vmem_limit_bytes=1 << 20),
     )(*outs)
     return hist3, hist4, leaf_values, new_pred.reshape(rows), new_weight.reshape(rows)

time: 29.2 us -> 26.6 us (0.911)
  Pallas kernels: 28.5 us -> 25.8 us
    pallas_call x1, Pallas kernels: 27.2 us -> 25.1 us  [on_device(): pl.pallas_call(functools.partial(kernel, total_rows, own), name='grow', i...]
    pallas_call x1, Pallas kernels: 1.26 us -> 0.76 us  [on_device(): pl.pallas_call(store_kernel, name='store', in_specs=[anywhere] * len(outs...]
where the time goes in v3:
time: 26.6 us; the launch traced here: 26.5 us
  Pallas kernels  25.8 us (97%)
  between operations  0.64 us (2%)
    pallas_call x1, Pallas kernels, on_device(): pl.pallas_call(functools.partial(kernel, total_rows, own), name='grow', i...  25.1 us
    pallas_call x1, Pallas kernels, on_device(): pl.pallas_call(store_kernel, name='store', in_specs=[anywhere] * len(outs...  0.76 us

profile of v3, /device:TPU:1, one launch (start us, length us, event | category | flops | bytes accessed | tf_op | source)
XLA Modules:
  0.0 26.5 jit_solution(16298866400192402621)
XLA Ops:
  0.6 25.1 %grow.1 = (f32[4,16,256]{2,1,0:T(8,128)S(1)}, f32[4,32,256]{2,1,0:T(8,128)S(1)}, f32[32]{0:T(128)S(1)}, f32[120,128]{1,0:T(8,128)S(1)}, f32[120,128]{1,0:T(8,128)S(1)}) custom-call(s32[8]{0:T(128)} %f3_hbm.1, s32[8]{0:T(128)} %b3_hbm.1, s32[16]{0:T(128)} %f4_hbm.1, s32[16]{0:T(128)} %b4_hbm.1, s32[2,960,128]{2,1,0:T(8,128)} %bitcast.11, ...), custom_call_target="tpu_custom_call" | custom-call | tf_op jit(solution)/shard_map/grow/pallas_call | solution.py:378
  25.7 0.8 %store.1 = (f32[4,16,256]{2,1,0:T(8,128)}, f32[4,32,256]{2,1,0:T(8,128)}, f32[32]{0:T(128)}, f32[120,128]{1,0:T(8,128)}, f32[120,128]{1,0:T(8,128)}) custom-call(f32[4,16,256]{2,1,0:T(8,128)S(1)} %get-tuple-element.15.refs_0_, f32[4,32,256]{2,1,0:T(8,128)S(1)} %get-tuple-element.16.refs_1_, f32[32]{0:T(128)S(1)} %get-tuple-element.17.refs_2_, ...), custom_call_target="tpu_custom_call" | custom-call | tf_op jit(solution)/shard_map/store/pallas_call | solution.py:427

commit v4 on v3

--- a/solution.py
+++ b/solution.py
@@ -15,6 +15,8 @@
 LANES = 128
 CHUNKS = 3
 GROUP = 8
+GROUP_ORDER = (5, 4, 7, 6, 3, 2, 1)
+LINE_ORDER = (4, 5, 3, 7, 6, 2, 1)
 MESH = pl.DeviceIdType.MESH
 F32 = jnp.float32
 BF16 = jnp.bfloat16
@@ -64,6 +66,7 @@
     low_ref,
     wr_ref,
     sr_ref,
+    node4_ref,
     leaf_ref,
     leafrow_ref,
     stat_ref,
@@ -79,7 +82,6 @@
     rs_sem,
     ar_sem,
     ag_sem,
-    leaf_send_sem,
     leaf_sem,
     in_sem,
     code_sem,
@@ -93,36 +95,31 @@
     in_group = [(plane * GROUP + flipped(group, j), feat) for j in range(1, GROUP)]
     in_line = [(flipped(plane, j) * GROUP + group, feat) for j in range(1, GROUP)]
 
+    def fetch(source, target, sem):
+        copy = pltpu.make_async_copy(source, target, sem)
+        copy.start()
+        return copy
+
+    part = tiles * 8 // CHUNKS
+    for a, b in ((node_hbm, node_ref), (weight_hbm, weight_ref), (label_hbm, label_ref)):
+        fetch(a, b, in_sem.at[4])
+    tables = ((f3_hbm, f3_ref), (b3_hbm, b3_ref), (f4_hbm, f4_ref), (b4_hbm, b4_ref))
+    ready = [fetch(a, b, in_sem.at[i]) for i, (a, b) in enumerate(tables)]
+    for c in range(CHUNKS):
+        rows = pl.ds(c * part, part)
+        fetch(codes_hbm.at[:, rows], codes_ref.at[:, rows], code_sem.at[c])
+    pred_ready = fetch(pred_hbm, pred_ref, in_sem.at[5])
+
     barrier = pltpu.get_barrier_semaphore()
     with jax.named_scope('signal'):
         for peer in in_group + in_line:
             pl.semaphore_signal(barrier, inc=1, device_id=peer, device_id_type=MESH)
 
-    def fetch(source, target, sem):
-        copy = pltpu.make_async_copy(source, target, sem)
-        copy.start()
-        return copy
-
-    part = tiles * 8 // CHUNKS
-    pieces = [pl.ds(c * part, part) for c in range(CHUNKS)]
-    small = [
-        (f3_hbm, f3_ref),
-        (b3_hbm, b3_ref),
-        (f4_hbm, f4_ref),
-        (b4_hbm, b4_ref),
-        (node_hbm, node_ref),
-        (label_hbm, label_ref),
-        (weight_hbm, weight_ref),
-        (pred_hbm, pred_ref),
-    ]
-    ready = [fetch(a, b, in_sem.at[i]) for i, (a, b) in enumerate(small[:5])]
-    for c in range(CHUNKS):
-        fetch(codes_hbm.at[:, pieces[c]], codes_ref.at[:, pieces[c]], code_sem.at[c])
-        if c == 0:
-            ready += [fetch(a, b, in_sem.at[5 + i]) for i, (a, b) in enumerate(small[5:])]
-    for i, copy in enumerate(ready):
-        with jax.named_scope('inwait%d' % i):
+    with jax.named_scope('inwait'):
+        for copy in ready:
             copy.wait()
+        whole = stat_ref.at[pl.ds(0, 3 * tiles)]
+        pltpu.make_async_copy(whole, whole, in_sem.at[4]).wait()
 
     features3 = [f3_ref[i] for i in range(NODES3)]
     bins3 = [b3_ref[i] for i in range(NODES3)]
@@ -136,42 +133,42 @@
             outs = [jnp.where(hit, table[i], out) for table, out in zip(tables, outs)]
         return outs
 
+    def side(step, node_of, features, bins):
+        codes = [codes_ref[f // 8, pl.ds(step * 64 + f % 8, 8, stride=8), :] for f in range(FEATURES)]
+        chosen, cutoff = lookup(node_of, [features, bins])
+        picked = codes[0]
+        for f in range(1, FEATURES):
+            picked = jnp.where(chosen == f, codes[f], picked)
+        return 2 * node_of + jnp.where(picked > cutoff, 1, 0)
+
     def route(step, carry):
         rows = pl.ds(step * 8, 8)
-        node = node_ref[rows, :]
-        codes = [
-            codes_ref[f // 8, pl.ds(step * 64 + f % 8, 8, stride=8), :]
-            for f in range(FEATURES)
-        ]
-
-        def side(node_of, features, bins):
-            chosen, cutoff = lookup(node_of, [features, bins])
-            picked = codes[0]
-            for f in range(1, FEATURES):
-                picked = jnp.where(chosen == f, codes[f], picked)
-            return 2 * node_of + jnp.where(picked > cutoff, 1, 0)
-
-        node4 = side(node, features3, bins3)
-        leaf = side(node4, features4, bins4)
-        leaf_ref[rows, :] = leaf
-        leafrow_ref[rows, :] = leaf.astype(F32)
+        node4 = side(step, node_ref[rows, :], features3, bins3)
+        node4_ref[rows, :] = node4
         for f in range(own_features):
             index = feat * own_features + f
             code = codes_ref[index // 8, pl.ds(step * 64 + index % 8, 8, stride=8), :]
             low_ref[f, rows, :] = (code & (LANES - 1)).astype(F32)
             key_ref[f, rows, :] = (node4 + NODES4 * (code >> 7)).astype(F32)
         weight = weight_ref[rows, :]
-        label = label_ref[rows, :]
-        rounded = weight.astype(BF16).astype(F32)
-        wr_ref[rows, :] = rounded
-        sr_ref[rows, :] = (weight * label).astype(BF16).astype(F32)
+        wr_ref[rows, :] = weight.astype(BF16).astype(F32)
+        sr_ref[rows, :] = (weight * label_ref[rows, :]).astype(BF16).astype(F32)
+        return carry
+
+    def leaf_route(step, carry):
+        rows = pl.ds(step * 8, 8)
+        leaf = side(step, node4_ref[rows, :], features4, bins4)
+        leaf_ref[rows, :] = leaf
+        leafrow_ref[rows, :] = leaf.astype(F32)
+        weight = weight_ref[rows, :]
+        positive = label_ref[rows, :] > 0.0
+        rounded = wr_ref[rows, :]
         rest = weight - rounded
         middle = rest.astype(BF16).astype(F32)
         low = rest - middle
-        positive = label > 0.0
-        for j, part in enumerate((rounded, middle, low)):
-            stat_ref[pl.ds(step * 64 + j, 8, stride=8), :] = jnp.where(positive, part, 0.0)
-            stat_ref[pl.ds(step * 64 + 3 + j, 8, stride=8), :] = jnp.where(positive, 0.0, part)
+        for j, term in enumerate((rounded, middle, low)):
+            stat_ref[pl.ds(step * 64 + j, 8, stride=8), :] = jnp.where(positive, term, 0.0)
+            stat_ref[pl.ds(step * 64 + 3 + j, 8, stride=8), :] = jnp.where(positive, 0.0, term)
         for j in (6, 7):
             stat_ref[pl.ds(step * 64 + j, 8, stride=8), :] = jnp.zeros((8, LANES), F32)
         return carry
@@ -207,27 +204,31 @@
             )
         return acc + dot_nt(jnp.concatenate(left, axis=1), jnp.concatenate(right, axis=1))
 
-    def send(source, target, sem, recv, peer):
+    def send(source, target, recv, peer):
         pltpu.make_async_remote_copy(
-            src_ref=source, dst_ref=target, send_sem=sem, recv_sem=recv, device_id=peer, device_id_type=MESH
+            src_ref=source, dst_ref=target, send_sem=send_sem, recv_sem=recv, device_id=peer, device_id_type=MESH
         ).start()
 
     def arrived(ref, sem):
         pltpu.make_async_copy(ref, ref, sem).wait()
 
+    others = pl.ds(1, GROUP - 1)
+    own_rows = pl.ds(pl.multiple_of(group * 8, 8), 8)
+
     def leaf_scatter():
+        lax.fori_loop(0, steps, leaf_route, 0, unroll=3)
         leaf_sums = lax.fori_loop(0, steps, leaf_step, jnp.zeros((8, LEAVES), F32), unroll=5)
         leaf_a_ref[0, :, :] = jnp.zeros((8, LANES), F32)
         leaf_a_ref[0, :, :LEAVES] = leaf_sums
-        for j in range(1, GROUP):
-            send(leaf_a_ref.at[0], leaf_a_ref.at[j], leaf_send_sem.at[0], leaf_sem.at[0], in_group[j - 1])
+        for j in GROUP_ORDER:
+            send(leaf_a_ref.at[0], leaf_a_ref.at[j], leaf_sem.at[0], in_group[j - 1])
 
     def leaf_exchange():
         with jax.named_scope('leafwait1'):
-            arrived(leaf_a_ref.at[pl.ds(1, GROUP - 1)], leaf_sem.at[0])
+            arrived(leaf_a_ref.at[others], leaf_sem.at[0])
         leaf_b_ref[0, :, :] = tree_sum([leaf_a_ref[j] for j in range(GROUP)])
-        for j in range(1, GROUP):
-            send(leaf_b_ref.at[0], leaf_b_ref.at[j], leaf_send_sem.at[1], leaf_sem.at[1], in_line[j - 1])
+        for j in LINE_ORDER:
+            send(leaf_b_ref.at[0], leaf_b_ref.at[j], leaf_sem.at[1], in_line[j - 1])
 
     def hist_step(f, step, acc):
         left, right = [], []
@@ -251,66 +252,55 @@
         acc_ref[f, :, :] = lax.fori_loop(
             0, steps, functools.partial(hist_step, f), jnp.zeros((LANES, 64), F32), unroll=15
         ).T
-        rs_ref[f, 0, :, :] = acc_ref[f, pl.ds(pl.multiple_of(group * 8, 8), 8), :]
-
-    def scatter(f):
-        for j in range(1, GROUP):
+
+    def scatter(c, first, count):
+        some = pl.ds(first, count)
+        for j in GROUP_ORDER:
             rows = pl.ds(pl.multiple_of(flipped(group, j) * 8, 8), 8)
-            send(acc_ref.at[f, rows], rs_ref.at[f, j], send_sem.at[f, 0], rs_sem.at[f], in_group[j - 1])
-
-    def exchange(f):
-        arrived(rs_ref.at[f, pl.ds(1, GROUP - 1)], rs_sem.at[f])
-        ar_ref[f, 0, :, :] = tree_sum([rs_ref[f, j] for j in range(GROUP)])
-        for j in range(1, GROUP):
-            send(ar_ref.at[f, 0], ar_ref.at[f, j], send_sem.at[f, 1], ar_sem.at[f], in_line[j - 1])
-
-    def gather(f):
-        arrived(ar_ref.at[f, pl.ds(1, GROUP - 1)], ar_sem.at[f])
-        mid_ref[f, :, :] = tree_sum([ar_ref[f, j] for j in range(GROUP)])
-        rows = pl.ds(pl.multiple_of(group * 8, 8), 8)
-        tot_ref[f, rows, :] = mid_ref[f, :, :]
-        for j in range(1, GROUP):
-            send(mid_ref.at[f], tot_ref.at[f, rows], send_sem.at[f, 2], ag_sem.at[f], in_group[j - 1])
-
-    def grow_feature(f, carry):
+            send(acc_ref.at[some, rows], rs_ref.at[j, some], rs_sem.at[c], in_group[j - 1])
+        rs_ref[0, some, :, :] = acc_ref[some, own_rows, :]
+
+    def exchange(c, first, count):
+        some = pl.ds(first, count)
+        with jax.named_scope('rswait'):
+            arrived(rs_ref.at[others, some], rs_sem.at[c])
+        ar_ref[0, some, :, :] = tree_sum([rs_ref[j, some] for j in range(GROUP)])
+        for j in LINE_ORDER:
+            send(ar_ref.at[0, some], ar_ref.at[j, some], ar_sem.at[c], in_line[j - 1])
+
+    def gather(c, first, count):
+        some = pl.ds(first, count)
+        with jax.named_scope('arwait'):
+            arrived(ar_ref.at[others, some], ar_sem.at[c])
+        mid_ref[some, :, :] = tree_sum([ar_ref[j, some] for j in range(GROUP)])
+        for j in GROUP_ORDER:
+            send(mid_ref.at[some], tot_ref.at[some, own_rows], ag_sem.at[c], in_group[j - 1])
+        tot_ref[some, own_rows, :] = mid_ref[some, :, :]
+
+    with jax.named_scope('compute'):
+        compute(0)
+        compute(1)
+    with jax.named_scope('barwait'):
+        pl.semaphore_wait(barrier, 2 * (GROUP - 1))
+    scatter(0, 0, 2)
+
+    def grow_one(f, carry):
         with jax.named_scope('compute'):
             compute(f)
-
-        @pl.when(f == 1)
-        def _():
-            with jax.named_scope('barwait'):
-                pl.semaphore_wait(barrier, 2 * (GROUP - 1))
-            scatter(0)
-
-        @pl.when(f >= 1)
-        def _():
-            scatter(f)
-
+        scatter(f - 1, f, 1)
         return carry
 
-    lax.fori_loop(0, own_features, grow_feature, 0)
-    with jax.named_scope('exchange0'):
-        exchange(0)
-    with jax.named_scope('exchange1'):
-        exchange(1)
+    lax.fori_loop(2, own_features, grow_one, 0)
+    batches = ((0, 0, 2), (1, 2, 1), (2, 3, 1))
     with jax.named_scope('leaf_scatter'):
         leaf_scatter()
-    with jax.named_scope('exchange2'):
-        exchange(2)
-    with jax.named_scope('exchange3'):
-        exchange(3)
-    with jax.named_scope('leaf_exchange'):
-        leaf_exchange()
-    with jax.named_scope('gather0'):
-        gather(0)
-    with jax.named_scope('gather1'):
-        gather(1)
-    with jax.named_scope('gather2'):
-        gather(2)
-    with jax.named_scope('gather3'):
-        gather(3)
+    for batch in batches:
+        exchange(*batch)
+    leaf_exchange()
+    for batch in batches:
+        gather(*batch)
     with jax.named_scope('leafwait2'):
-        arrived(leaf_b_ref.at[pl.ds(1, GROUP - 1)], leaf_sem.at[1])
+        arrived(leaf_b_ref.at[others], leaf_sem.at[1])
     leaf_mid_ref[...] = tree_sum([leaf_b_ref[j] for j in range(GROUP)])
     plus = leaf_mid_ref[0:1, :]
     minus = leaf_mid_ref[3:4, :]
@@ -330,29 +320,24 @@
         new_weight_ref[rows, :] = raw * scale
         return carry
 
+    pred_ready.wait()
     with jax.named_scope('update'):
         lax.fori_loop(0, steps, update, 0, unroll=5)
 
-    everything = pl.ds(1, GROUP - 1)
+    for c, first, count in batches:
+        with jax.named_scope('agwait'):
+            arrived(tot_ref.at[pl.ds(first, count), pl.ds(0, 8 * (GROUP - 1))], ag_sem.at[c])
+        for f in range(first, first + count):
+            for hi in range(2):
+                lanes = slice(hi * LANES, (hi + 1) * LANES)
+                base = hi * 2 * NODES4
+                hist4_ref[f, :, lanes] = tot_ref[f, base : base + 2 * NODES4, :]
+                even = tot_ref[f, pl.ds(base, 2 * NODES3, stride=2), :]
+                odd = tot_ref[f, pl.ds(base + 1, 2 * NODES3, stride=2), :]
+                hist3_ref[f, :, lanes] = even + odd
+    sent = (3 * own_features + 2) * (GROUP - 1) * 8
     with jax.named_scope('sendwait'):
-        for f in range(own_features):
-            arrived(rs_ref.at[f, everything], send_sem.at[f, 0])
-            arrived(ar_ref.at[f, everything], send_sem.at[f, 1])
-        arrived(leaf_a_ref.at[everything], leaf_send_sem.at[0])
-        arrived(leaf_b_ref.at[everything], leaf_send_sem.at[1])
-    for f in range(own_features):
-        with jax.named_scope('agwait'):
-            arrived(tot_ref.at[f, pl.ds(0, 8 * (GROUP - 1))], ag_sem.at[f])
-        for hi in range(2):
-            lanes = slice(hi * LANES, (hi + 1) * LANES)
-            base = hi * 2 * NODES4
-            hist4_ref[f, :, lanes] = tot_ref[f, base : base + 2 * NODES4, :]
-            even = tot_ref[f, pl.ds(base, 2 * NODES3, stride=2), :]
-            odd = tot_ref[f, pl.ds(base + 1, 2 * NODES3, stride=2), :]
-            hist3_ref[f, :, lanes] = even + odd
-    with jax.named_scope('sendwait'):
-        for f in range(own_features):
-            arrived(tot_ref.at[f, pl.ds(0, 8 * (GROUP - 1))], send_sem.at[f, 2])
+        arrived(codes_ref.at[0, pl.ds(0, sent)], send_sem)
 
 
 def store_kernel(*refs):
@@ -402,23 +387,23 @@
             pltpu.VMEM((tiles, LANES), F32),
             pltpu.VMEM((tiles, LANES), F32),
             pltpu.VMEM((tiles, LANES), jnp.int32),
+            pltpu.VMEM((tiles, LANES), jnp.int32),
             pltpu.VMEM((tiles, LANES), F32),
             pltpu.VMEM((tiles * 8, LANES), F32),
             pltpu.VMEM((own, 64, LANES), F32),
-            pltpu.VMEM((own, GROUP, 8, LANES), F32),
+            pltpu.VMEM((GROUP, own, 8, LANES), F32),
             pltpu.VMEM((own, 8, LANES), F32),
-            pltpu.VMEM((own, GROUP, 8, LANES), F32),
+            pltpu.VMEM((GROUP, own, 8, LANES), F32),
             pltpu.VMEM((own, 64, LANES), F32),
             pltpu.VMEM((GROUP, 8, LANES), F32),
             pltpu.VMEM((GROUP, 8, LANES), F32),
             pltpu.VMEM((8, LANES), F32),
-            pltpu.SemaphoreType.DMA((own, 3)),
-            pltpu.SemaphoreType.DMA((own,)),
-            pltpu.SemaphoreType.DMA((own,)),
-            pltpu.SemaphoreType.DMA((own,)),
+            pltpu.SemaphoreType.DMA(()),
+            pltpu.SemaphoreType.DMA((3,)),
+            pltpu.SemaphoreType.DMA((3,)),
+            pltpu.SemaphoreType.DMA((3,)),
             pltpu.SemaphoreType.DMA((2,)),
-            pltpu.SemaphoreType.DMA((2,)),
-            pltpu.SemaphoreType.DMA((8,)),
+            pltpu.SemaphoreType.DMA((6,)),
             pltpu.SemaphoreType.DMA((CHUNKS,)),
         ],
         compiler_params=pltpu.CompilerParams(collective_id=0, has_side_effects=True, vmem_limit_bytes=16 << 20),

time: 26.6 us -> 25.3 us (0.951)
  Pallas kernels: 25.8 us -> 24.6 us
    pallas_call x1, Pallas kernels: 25.1 us -> 23.8 us  [on_device(): pl.pallas_call(functools.partial(kernel, total_rows, own), name='grow', i...]
where the time goes in v4:
time: 25.3 us; the launch traced here: 25.2 us
  Pallas kernels  24.6 us (97%)
  between operations  0.64 us (3%)
    pallas_call x1, Pallas kernels, on_device(): pl.pallas_call(functools.partial(kernel, total_rows, own), name='grow', i...  23.8 us
    pallas_call x1, Pallas kernels, on_device(): pl.pallas_call(store_kernel, name='store', in_specs=[anywhere] * len(outs...  0.76 us

profile of v4, /device:TPU:1, one launch (start us, length us, event | category | flops | bytes accessed | tf_op | source)
XLA Modules:
  0.0 25.2 jit_solution(14363600939760513859)
XLA Ops:
  0.6 23.8 %grow.1 = (f32[4,16,256]{2,1,0:T(8,128)S(1)}, f32[4,32,256]{2,1,0:T(8,128)S(1)}, f32[32]{0:T(128)S(1)}, f32[120,128]{1,0:T(8,128)S(1)}, f32[120,128]{1,0:T(8,128)S(1)}) custom-call(s32[8]{0:T(128)} %f3_hbm.1, s32[8]{0:T(128)} %b3_hbm.1, s32[16]{0:T(128)} %f4_hbm.1, s32[16]{0:T(128)} %b4_hbm.1, s32[2,960,128]{2,1,0:T(8,128)} %bitcast.11, ...), custom_call_target="tpu_custom_call" | custom-call | tf_op jit(solution)/shard_map/grow/pallas_call | solution.py:363
  24.5 0.8 %store.1 = (f32[4,16,256]{2,1,0:T(8,128)}, f32[4,32,256]{2,1,0:T(8,128)}, f32[32]{0:T(128)}, f32[120,128]{1,0:T(8,128)}, f32[120,128]{1,0:T(8,128)}) custom-call(f32[4,16,256]{2,1,0:T(8,128)S(1)} %get-tuple-element.15.refs_0_, f32[4,32,256]{2,1,0:T(8,128)S(1)} %get-tuple-element.16.refs_1_, f32[32]{0:T(128)S(1)} %get-tuple-element.17.refs_2_, ...), custom_call_target="tpu_custom_call" | custom-call | tf_op jit(solution)/shard_map/store/pallas_call | solution.py:412
